TPU v7x, 512 devices: a whole 4x4x16 slice. The times are simulated.
512 devices in a mesh: region: 16 (over y, x), tile: 32 (over z, core).
Axes of the slice: x: 4, y: 4, z: 16, core: 2. Of those that a mesh axis runs over, the one named last changes fastest.
Arguments:
- density: float32 [16, 1024, 1024], P('region', 'tile'), may hold values from -48 to 56, as said below
- atom_xyz: float32 [16, 3, 256], P('region'), may hold values from 0 to 3
- atom_of: int32 [16, 1024], P('region'), may hold values from 0 to 255
- exponent: float32 [16, 1024], P('region'), may hold values from 0.1 to 1
- points: float32 [1024, 3, 512], P(('region', 'tile')), may hold values from 0 to 3
- weights: float32 [1024, 512], P(('region', 'tile')), may hold values from 6.1035156e-05 to 0.00018310547
- lists: int32 [1024, 4], P(('region', 'tile')), may hold values from 0 to 7, all different within a row
- live: int32 [512], P(('region', 'tile')), may hold values from 1 to 2, as said below
Outputs:
- potential: float32 [16, 1024, 1024], P('region', 'tile')
Inputs may be any that keep to these rules, and one draw needn't show every extreme that they name: `density`: each region's matrix is symmetric and positive definite. `lists`: each row names 4 different blocks of its own region. a device's slots 0 to live - 1 hold its live batches and the others are unused; some device has 2.
All inputs are finite; a program needn't handle non-finite values.
Results may differ from a plain program's by a relative error of at most 0.0003.
Values sent between devices are 32-bit elements; how exact they have to be, the bound alone decides.
No kernel may reach another device: no remote copies, remote signals or barrier semaphores. Data moves between devices by JAX's collectives and lax.ppermute only.
A program may use at most 128 MiB of HBM per device.

v0:
```python
import math
import jax
import jax.numpy as jnp
from jax import lax
from jax.sharding import Mesh
from jax.sharding import PartitionSpec as P

BLK = 128
TILE = ("tile_0", "tile_1")
REGION_TILE = ("region", "tile_0", "tile_1")
slater_coef = (3.0 / math.pi) ** (1.0 / 3.0)
highest = lax.Precision.HIGHEST


def reduced_to_own(tiles, axes, turns):
    lengths = [lax.axis_size(a) for a in axes]
    tiles = tiles.reshape(*lengths, *tiles.shape[1:])
    tiles = tiles.transpose(*turns, *range(len(axes), tiles.ndim))
    tiles = tiles.reshape(-1, *tiles.shape[len(axes) :])
    for k in turns:
        tiles = lax.psum_scatter(tiles, axes[k], scatter_dimension=0, tiled=True)
    return tiles[0]


def cut_along(value, dim, size):
    lengths = value.shape
    tiles = value.reshape(*lengths[:dim], size, lengths[dim] // size, *lengths[dim + 1 :])
    return jnp.moveaxis(tiles, dim, 0)


def scatter_axes(value, axes, turns, dim):
    size = lax.axis_size(axes)
    return reduced_to_own(cut_along(value, dim, size), axes, turns)


def expand_blocks(blocks):
    inner = jnp.arange(BLK, dtype=jnp.int32)
    full = blocks[..., :, None] * BLK + inner
    return full.reshape(blocks.shape[:-1] + (blocks.shape[-1] * BLK,))


def gather_block(region_density, blocks):
    block_total = region_density.shape[0] // BLK
    count = blocks.shape[0]
    tiled = region_density.reshape(block_total, BLK, block_total, BLK)
    picked = jnp.take(jnp.take(tiled, blocks, axis=0), blocks, axis=2)
    return picked.reshape(count * BLK, count * BLK)


def add_term(running, blocks, batch_result):
    block_total = running.shape[1] // BLK
    count = blocks.shape[0]
    pieces = batch_result.reshape(count, BLK, count, BLK)
    for row_block in range(count):
        start = blocks[row_block] * BLK
        slab = lax.dynamic_slice_in_dim(running, start, BLK, 0).reshape(BLK, block_total, BLK)
        slab = slab.at[:, blocks, :].add(pieces[row_block])
        running = lax.dynamic_update_slice_in_dim(
            running, slab.reshape(BLK, block_total * BLK), start, 0
        )
    return running


def orbital_matrix(coords, centers, exponents):
    distance = jnp.zeros((coords.shape[1], centers.shape[1]), jnp.float32)
    for axis_no in range(3):
        offset = coords[axis_no][:, None] - centers[axis_no][None, :]
        distance = distance + offset * offset
    return jnp.exp(-exponents[None, :] * distance)


def batch_term(coords, weight, centers, exponents, block_density):
    orbital = orbital_matrix(coords, centers, exponents)
    mixed = jnp.dot(orbital, block_density, precision=highest, preferred_element_type=jnp.float32)
    point_density = jnp.sum(orbital * mixed, axis=1)
    factor = weight * -slater_coef * jnp.cbrt(point_density)
    return lax.dot_general(
        orbital,
        orbital * factor[:, None],
        (((0,), (0,)), ((), ())),
        precision=highest,
        preferred_element_type=jnp.float32,
    )


def body(density, atom_xyz, atom_of, exponent, points, weights, lists, live):
    table_xyz = atom_xyz[0]
    atom_index = atom_of[0]
    exponent_row = exponent[0]
    region_density = lax.all_gather(density, TILE, axis=1, tiled=True)[0]
    members_all = expand_blocks(lists)
    centers = jnp.moveaxis(jnp.take(table_xyz, jnp.take(atom_index, members_all), axis=1), 1, 0)
    exponents = jnp.take(exponent_row, members_all)
    own_count = live[0]
    running = jnp.zeros(region_density.shape, jnp.float32)

    def own_batch(slot_no, running):
        blocks = lists[slot_no]
        batch_result = batch_term(
            points[slot_no],
            weights[slot_no],
            centers[slot_no],
            exponents[slot_no],
            gather_block(region_density, blocks),
        )
        return add_term(running, blocks, batch_result)

    running = lax.fori_loop(0, own_count, own_batch, running)
    owned_rows = scatter_axes(running[None], TILE, (1, 0), 1)
    return owned_rows


def solution(mesh):
    torus = Mesh(mesh.devices.reshape(mesh.shape["region"], 16, 2), ("region", "tile_0", "tile_1"))
    return jax.shard_map(
        body,
        mesh=torus,
        in_specs=(
            P("region", TILE, None),
            P("region", None, None),
            P("region", None),
            P("region", None),
            P(REGION_TILE, None, None),
            P(REGION_TILE, None),
            P(REGION_TILE, None),
            P(REGION_TILE),
        ),
        out_specs=P("region", TILE, None),
        check_vma=False,
    )
```

profile of v0, /device:TPU:8, one launch (start us, length us, event | category | flops | bytes accessed | tf_op | source)
XLA Modules:
  0.0 269.8 jit_solution(4212617765108527290)
XLA Ops:
  8.1 4.5 %gather_fusion.3 = s32[1024]{0:T(1024)S(1)} fusion(s32[1024]{0:T(1024)S(1)} %bitcast.149, s32[1024]{0:T(1024)S(1)} %broadcast_clamp_fusion.1), kind=kCustom, calls=%fused_computation.3 | custom fusion | bytes 12288 | tf_op jit(solution)/shard_map/jit(_take)/gather | solution.py:92
  12.9 2.8 %gather_fusion.4 = f32[1024,3]{1,0:T(8,128)S(1)} fusion(f32[3,256]{0,1:T(8,128)S(1)} %bitcast.174, s32[1024]{0:T(1024)S(1)} %broadcast_clamp_fusion), kind=kCustom, calls=%fused_computation.4 | custom fusion | bytes 28672 | tf_op jit(solution)/shard_map/jit(_take)/gather | solution.py:92
  15.9 4.5 %gather_fusion.2 = f32[1024]{0:T(1024)S(1)} fusion(f32[1024]{0:T(1024)S(1)} %bitcast.150, s32[1024]{0:T(1024)S(1)} %broadcast_clamp_fusion.1), kind=kCustom, calls=%fused_computation.2 | custom fusion | bytes 12288 | tf_op jit(solution)/shard_map/jit(_take)/gather | solution.py:93
  20.6 66.7 %all-gather.2.cloned.1.call-done = f32[1,1024,1024]{2,1,0:T(8,128)} async-done(((f32[1,32,1024]{2,1,0:T(8,128)}), f32[1,1024,1024]{2,1,0:T(8,128)}) %all-gather.2.cloned.1.call-update) | async-done | bytes 4194320 | tf_op jit(solution)/shard_map/all_gather | solution.py:90
  87.2 2.5 broadcast_in_dim.58
  89.8 65.6 %while.10 = (s32[]{:T(128)}, f32[1024,1024]{0,1:T(8,128)}, s32[]{:T(128)}, s32[2,4]{1,0:T(2,128)S(1)}, f32[2,512]{1,0:T(2,128)S(1)}, /*index=5*/f32[2,3,512]{2,0...) while((s32[]{:T(128)}, f32[1024,1024]{0,1:T(8,128)}, ...), condition=%wide.region_6.7_spmd, body=%wide.region_0.6_spmd.sunk | while | flops 3230140416 | bytes 51457692 | solution.py:108
  90.5 5.1 %copy.95 = f32[128,8,8,128]{3,2,1,0:T(8,128)} copy(f32[128,8,8,128]{3,1,2,0:T(8,128)} %bitcast.152) | data formatting | bytes 8388608 | tf_op jit(solution)/shard_map/while
  95.6 2.9 %gather_fusion = f32[4,128,8,128]{3,2,1,0:T(8,128)S(1)} fusion(f32[8,128,8,128]{3,2,1,0:T(8,128)} %bitcast.151, s32[1024]{0:T(1024)S(1)} %pad_clamp_fusion.2), kind=kCustom, calls=%fused_computation.clone.1 | custom fusion | bytes 4194320 | tf_op jit(solution)/shard_map/while/body/jit(_take)/gather | solution.py:46
  100.5 2.6 fusion.40
  103.2 2.7 fusion.41
  107.4 1.1 constant_dynamic-slice_fusion.20
  109.6 0.9 constant_dynamic-update-slice_fusion.8
  111.2 1.1 constant_dynamic-slice_fusion.23
  113.6 0.9 constant_dynamic-update-slice_fusion.9
  115.0 1.1 constant_dynamic-slice_fusion.24
  117.4 0.9 constant_dynamic-update-slice_fusion.10
  118.9 1.1 constant_dynamic-slice_fusion.25
  121.3 0.9 constant_dynamic-update-slice_fusion.11
  122.9 5.1 %copy.95 = f32[128,8,8,128]{3,2,1,0:T(8,128)} copy(f32[128,8,8,128]{3,1,2,0:T(8,128)} %bitcast.152) | data formatting | bytes 8388608 | tf_op jit(solution)/shard_map/while
  128.1 2.9 %gather_fusion = f32[4,128,8,128]{3,2,1,0:T(8,128)S(1)} fusion(f32[8,128,8,128]{3,2,1,0:T(8,128)} %bitcast.151, s32[1024]{0:T(1024)S(1)} %pad_clamp_fusion.2), kind=kCustom, calls=%fused_computation.clone.1 | custom fusion | bytes 4194320 | tf_op jit(solution)/shard_map/while/body/jit(_take)/gather | solution.py:46
  133.0 2.6 fusion.40
  135.7 2.7 fusion.41
  139.8 1.1 constant_dynamic-slice_fusion.20
  142.1 0.9 constant_dynamic-update-slice_fusion.8
  143.7 1.1 constant_dynamic-slice_fusion.23
  147.5 1.1 constant_dynamic-slice_fusion.24
  151.4 1.1 constant_dynamic-slice_fusion.25
  153.8 0.9 constant_dynamic-update-slice_fusion.11
  155.3 5.4 %copy.64 = f32[1024,1024]{1,0:T(8,128)} copy(f32[1024,1024]{0,1:T(8,128)} %get-tuple-element.53) | data formatting | bytes 8388608 | tf_op jit(solution)/shard_map/while | solution.py:108
  160.7 4.7 %copy.65 = f32[2,16,1,32,1024]{4,3,1,0,2:T(8,128)} copy(f32[2,16,1,32,1024]{4,3,0,1,2:T(8,128)} %bitcast.172) | data formatting | bytes 8388608 | tf_op jit(solution)/shard_map/transpose | solution.py:18
  165.5 19.4 %reduce-scatter.3.cloned.1.call-done = f32[16,1,32,1024]{3,2,0,1:T(8,128)} async-done(((f32[32,1,32,1024]{3,2,0,1:T(8,128)}), f32[16,1,32,1024]{3,2,0,1:T(8,128)}) %reduce-scatter.3.cloned.1.call-update) | async-done | bytes 2097168 | tf_op jit(solution)/shard_map/reduce_scatter | solution.py:21
  184.9 78.4 %reduce-scatter.5.cloned.1.call-done = f32[1,1,32,1024]{3,2,0,1:T(8,128)} async-done(((f32[16,1,32,1024]{3,2,0,1:T(8,128)}), f32[1,1,32,1024]{3,2,0,1:T(8,128)}) %reduce-scatter.5.cloned.1.call-update) | async-done | bytes 131088 | tf_op jit(solution)/shard_map/reduce_scatter | solution.py:21
  (99 shorter events, 19.6 us)
Async XLA Ops:
  6.5 1.6 copy-start
  6.5 6.2 %copy-start.5 = (f32[1,3,256]{2,0,1:T(1,128)S(1)}, f32[1,3,256]{2,0,1:T(1,128)}, u32[]{:S(2)}) copy-start(f32[1,3,256]{2,0,1:T(1,128)} %param.11) | copy-start | bytes 9220
  6.5 9.4 %copy-start.1 = (f32[1,1024]{1,0:T(1,128)S(1)}, f32[1,1024]{1,0:T(1,128)}, u32[]{:S(2)}) copy-start(f32[1,1024]{1,0:T(1,128)} %param.13) | copy-start | bytes 12292
  6.5 80.7 %all-gather.2.cloned.1.call-start = ((), (), s32[]{:S(2)}) async-start(), calls=%async_computation.2 | async-start | bytes 4325376 | tf_op jit(solution)/shard_map/all_gather | solution.py:90
  7.3 177.6 %reduce-scatter.3.cloned.1.call-start = ((), (), s32[]{:S(2)}) async-start(), calls=%async_computation.3 | async-start | bytes 6291456 | tf_op jit(solution)/shard_map/reduce_scatter | solution.py:21
  15.9 73.9 %copy-start.2 = (f32[2,3,512]{2,0,1:T(2,128)S(1)}, f32[2,3,512]{2,0,1:T(2,128)}, u32[]{:S(2)}) copy-start(f32[2,3,512]{2,0,1:T(2,128)} %param.14) | copy-start | bytes 36868
  15.9 73.9 %copy-start.3 = (f32[2,512]{1,0:T(2,128)S(1)}, f32[2,512]{1,0:T(2,128)}, u32[]{:S(2)}) copy-start(f32[2,512]{1,0:T(2,128)} %param.15) | copy-start | bytes 12292
  15.9 73.8 %copy-start.4 = (s32[2,4]{1,0:T(2,128)S(1)}, s32[2,4]{1,0:T(2,128)}, u32[]{:S(2)}) copy-start(s32[2,4]{1,0:T(2,128)} %param.16) | copy-start | bytes 100
  165.4 97.8 %reduce-scatter.5.cloned.1.call-start = ((), (), s32[]{:S(2)}) async-start(), calls=%async_computation.4 | async-start | bytes 2228224 | tf_op jit(solution)/shard_map/reduce_scatter | solution.py:21
Sparse Core Ops, SparseCore 0:
  9.5 77.7 all-gather.1
  165.6 19.2 reduce-scatter.2
  187.7 75.5 reduce-scatter.4
where the time goes:
time: 271 us; the launch traced here: 270 us
  waiting for transfers between devices  165 us (61%)
  local copies, waits for them, and re-layouts  65.9 us (24%)
  between operations  13.3 us (5%)
  matrix products  10.6 us (4%)
  loops' own time  7.47 us (3%)
  other arithmetic  7.3 us (3%)
    reduce_scatter x2, waiting for transfers between devices, reduced_to_own(): tiles = lax.psum_scatter(tiles, axes[k], scatter_dimension=0, tiled=True)  97.7 us
    all_gather x1, waiting for transfers between devices, body(): region_density = lax.all_gather(density, TILE, axis=1, tiled=True)[0]  66.7 us
    while x2, local copies, waits for them, and re-layouts  10.3 us
    dynamic_slice x8, local copies, waits for them, and re-layouts, add_term(): lax.dynamic_slice_in_dim(running, start, BLK, 0)  8.65 us
    gather x6, local copies, waits for them, and re-layouts, gather_block(): picked = jnp.take(jnp.take(tiled, blocks, axis=0), blocks, axis=2)  8.32 us
    another operation x1, loops' own time, body(): running = lax.fori_loop(0, own_count, own_batch, running)  7.47 us
    dynamic_update_slice x8, local copies, waits for them, and re-layouts, add_term(): lax.dynamic_update_slice_in_dim(running, slab.reshape(BLK, block_total *...  7.07 us
    scatter-add x8, other arithmetic, add_term(): slab = slab.at[:, blocks, :].add(pieces[row_block])  6.02 us
  transfers between devices with their start and end apart: 3, of which 3 were waited for; matrix products, arithmetic and copies ran while one was open for 5% of the time, Pallas kernels for 0%

commit v1 on v0

--- a/solution.py
+++ b/solution.py
@@ -87,7 +87,9 @@
     table_xyz = atom_xyz[0]
     atom_index = atom_of[0]
     exponent_row = exponent[0]
-    region_density = lax.all_gather(density, TILE, axis=1, tiled=True)[0]
+    region_density = jnp.concatenate(
+        lax.all_to_all(jnp.stack([density] * lax.axis_size(TILE)), TILE, 0, 0), axis=1
+    )[0]
     members_all = expand_blocks(lists)
     centers = jnp.moveaxis(jnp.take(table_xyz, jnp.take(atom_index, members_all), axis=1), 1, 0)
     exponents = jnp.take(exponent_row, members_all)

time: 271 us -> 395 us (1.46)
  the two profiles are of different devices: /device:TPU:8 before, /device:TPU:10 now
where the time goes in v1:
time: 395 us; the launch traced here: 394 us
  waiting for transfers between devices  271 us (69%)
  local copies, waits for them, and re-layouts  69.2 us (18%)
  starting transfers between devices  15.8 us (4%)
  between operations  13.6 us (3%)
  matrix products  10.6 us (3%)
  loops' own time  7.38 us (2%)
  other arithmetic  6.62 us (2%)
    all_to_all x1, waiting for transfers between devices, body(): lax.all_to_all(jnp.stack([density] * lax.axis_size(TILE)), TILE, 0, 0)  171 us
    reduce_scatter x2, waiting for transfers between devices, reduced_to_own(): tiles = lax.psum_scatter(tiles, axes[k], scatter_dimension=0, tiled=True)  100 us
    all_to_all x1, starting transfers between devices, body(): lax.all_to_all(jnp.stack([density] * lax.axis_size(TILE)), TILE, 0, 0)  15.7 us
    while x2, local copies, waits for them, and re-layouts  10.3 us
    dynamic_slice x8, local copies, waits for them, and re-layouts, add_term(): lax.dynamic_slice_in_dim(running, start, BLK, 0)  8.66 us
    gather x6, local copies, waits for them, and re-layouts, gather_block(): picked = jnp.take(jnp.take(tiled, blocks, axis=0), blocks, axis=2)  8.32 us
  transfers between devices with their start and end apart: 3, of which 3 were waited for; matrix products, arithmetic and copies ran while one was open for 3% of the time, Pallas kernels for 0%

profile of v1, /device:TPU:10, one launch (start us, length us, event | category | flops | bytes accessed | tf_op | source)
XLA Modules:
  0.0 394.1 jit_solution(7343746485088691261)
XLA Ops:
  6.5 3.4 stack.2
  9.9 15.7 %all-to-all-start = ((f32[32,1,32,1024]{3,2,1,0:T(8,128)}), f32[32,1,32,1024]{3,2,1,0:T(8,128)}, u32[]{:S(2)}, u32[]{:S(2)}) async-start(f32[32,1,32,1024]{3,2,1,0:T(8,128)} %stack.2), calls=%async_computation | async-start | bytes 8388608 | tf_op jit(solution)/shard_map/all_to_all | solution.py:91
  25.9 4.5 %gather_fusion.3 = s32[1024]{0:T(1024)S(1)} fusion(s32[1024]{0:T(1024)S(1)} %bitcast.153, s32[1024]{0:T(1024)S(1)} %broadcast_clamp_fusion.1), kind=kCustom, calls=%fused_computation.3 | custom fusion | bytes 12288 | tf_op jit(solution)/shard_map/jit(_take)/gather | solution.py:94
  30.7 2.8 gather_fusion.4
  33.7 4.5 %gather_fusion.2 = f32[1024]{0:T(1024)S(1)} fusion(f32[1024]{0:T(1024)S(1)} %bitcast.154, s32[1024]{0:T(1024)S(1)} %broadcast_clamp_fusion.1), kind=kCustom, calls=%fused_computation.2 | custom fusion | bytes 12288 | tf_op jit(solution)/shard_map/jit(_take)/gather | solution.py:95
  38.4 170.8 %all-to-all-done = f32[32,1,32,1024]{3,2,1,0:T(8,128)} async-done(((f32[32,1,32,1024]{3,2,1,0:T(8,128)}), f32[32,1,32,1024]{3,2,1,0:T(8,128)}, u32[]{:S(2)}, u32[]{:S(2)}) %all-to-all-start) | async-done | bytes 4194336 | tf_op jit(solution)/shard_map/all_to_all | solution.py:91
  209.2 2.5 broadcast_in_dim.58
  211.7 65.4 %while.10 = (s32[]{:T(128)}, f32[1024,1024]{0,1:T(8,128)}, s32[]{:T(128)}, s32[2,4]{1,0:T(2,128)S(1)}, f32[2,512]{1,0:T(2,128)S(1)}, /*index=5*/f32[2,3,512]{2,0...) while((s32[]{:T(128)}, f32[1024,1024]{0,1:T(8,128)}, ...), condition=%wide.region_6.7_spmd, body=%wide.region_0.6_spmd.sunk | while | flops 3230140416 | bytes 51457692 | solution.py:110
  212.4 5.2 %copy.114 = f32[128,8,8,128]{3,2,1,0:T(8,128)} copy(f32[128,8,8,128]{3,1,2,0:T(8,128)} %bitcast.124) | data formatting | bytes 8388608 | tf_op jit(solution)/shard_map/while
  217.5 2.9 gather_fusion
  222.5 2.6 fusion.40
  225.1 2.7 fusion.41
  229.3 1.1 constant_dynamic-slice_fusion.20
  231.6 0.9 constant_dynamic-update-slice_fusion.8
  233.0 1.1 constant_dynamic-slice_fusion.23
  236.9 1.1 constant_dynamic-slice_fusion.24
  240.8 1.1 constant_dynamic-slice_fusion.25
  243.1 0.9 constant_dynamic-update-slice_fusion.11
  244.8 5.2 %copy.114 = f32[128,8,8,128]{3,2,1,0:T(8,128)} copy(f32[128,8,8,128]{3,1,2,0:T(8,128)} %bitcast.124) | data formatting | bytes 8388608 | tf_op jit(solution)/shard_map/while
  249.9 2.9 gather_fusion
  254.8 2.6 fusion.40
  257.5 2.7 fusion.41
  261.7 1.1 constant_dynamic-slice_fusion.20
  263.9 0.9 constant_dynamic-update-slice_fusion.8
  265.4 1.1 constant_dynamic-slice_fusion.23
  269.3 1.1 constant_dynamic-slice_fusion.24
  271.6 0.9 constant_dynamic-update-slice_fusion.10
  273.1 1.1 constant_dynamic-slice_fusion.25
  277.1 5.4 %copy.83 = f32[1024,1024]{1,0:T(8,128)} copy(f32[1024,1024]{0,1:T(8,128)} %get-tuple-element.53) | data formatting | bytes 8388608 | tf_op jit(solution)/shard_map/while | solution.py:110
  282.4 4.7 %copy.84 = f32[2,16,1,32,1024]{4,3,1,0,2:T(8,128)} copy(f32[2,16,1,32,1024]{4,3,0,1,2:T(8,128)} %bitcast.175) | data formatting | bytes 8388608 | tf_op jit(solution)/shard_map/transpose | solution.py:18
  287.2 21.7 %reduce-scatter.3.cloned.1.call-done = f32[16,1,32,1024]{3,2,0,1:T(8,128)} async-done(((f32[32,1,32,1024]{3,2,0,1:T(8,128)}), f32[16,1,32,1024]{3,2,0,1:T(8,128)}) %reduce-scatter.3.cloned.1.call-update) | async-done | bytes 2097168 | tf_op jit(solution)/shard_map/reduce_scatter | solution.py:21
  308.9 78.3 %reduce-scatter.5.cloned.1.call-done = f32[1,1,32,1024]{3,2,0,1:T(8,128)} async-done(((f32[16,1,32,1024]{3,2,0,1:T(8,128)}), f32[1,1,32,1024]{3,2,0,1:T(8,128)}) %reduce-scatter.5.cloned.1.call-update) | async-done | bytes 131088 | tf_op jit(solution)/shard_map/reduce_scatter | solution.py:21
  (99 shorter events, 19.8 us)
Async XLA Ops:
  6.5 19.4 %copy-start = (s32[1,1024]{1,0:T(1,128)S(1)}, s32[1,1024]{1,0:T(1,128)}, u32[]{:S(2)}) copy-start(s32[1,1024]{1,0:T(1,128)} %param.12) | copy-start | bytes 12292
  9.9 15.8 %copy-start.4 = (s32[2,4]{1,0:T(2,128)S(1)}, s32[2,4]{1,0:T(2,128)}, u32[]{:S(2)}) copy-start(s32[2,4]{1,0:T(2,128)} %param.16) | copy-start | bytes 100
  9.9 199.2 %all-to-all-start = ((f32[32,1,32,1024]{3,2,1,0:T(8,128)}), f32[32,1,32,1024]{3,2,1,0:T(8,128)}, u32[]{:S(2)}, u32[]{:S(2)}) async-start(f32[32,1,32,1024]{3,2,1,0:T(8,128)} %stack.2), calls=%async_computation | async-start | bytes 8388608 | tf_op jit(solution)/shard_map/all_to_all | solution.py:91
  25.7 4.8 %copy-start.5 = (f32[1,3,256]{2,0,1:T(1,128)S(1)}, f32[1,3,256]{2,0,1:T(1,128)}, u32[]{:S(2)}) copy-start(f32[1,3,256]{2,0,1:T(1,128)} %param.11) | copy-start | bytes 9220
  25.7 8.0 %copy-start.1 = (f32[1,1024]{1,0:T(1,128)S(1)}, f32[1,1024]{1,0:T(1,128)}, u32[]{:S(2)}) copy-start(f32[1,1024]{1,0:T(1,128)} %param.13) | copy-start | bytes 12292
  25.7 283.2 %reduce-scatter.3.cloned.1.call-start = ((), (), s32[]{:S(2)}) async-start(), calls=%async_computation.3 | async-start | bytes 6291456 | tf_op jit(solution)/shard_map/reduce_scatter | solution.py:21
  33.7 178.0 %copy-start.2 = (f32[2,3,512]{2,0,1:T(2,128)S(1)}, f32[2,3,512]{2,0,1:T(2,128)}, u32[]{:S(2)}) copy-start(f32[2,3,512]{2,0,1:T(2,128)} %param.14) | copy-start | bytes 36868
  33.7 178.0 %copy-start.3 = (f32[2,512]{1,0:T(2,128)S(1)}, f32[2,512]{1,0:T(2,128)}, u32[]{:S(2)}) copy-start(f32[2,512]{1,0:T(2,128)} %param.15) | copy-start | bytes 12292
  287.2 100.1 %reduce-scatter.5.cloned.1.call-start = ((), (), s32[]{:S(2)}) async-start(), calls=%async_computation.4 | async-start | bytes 2228224 | tf_op jit(solution)/shard_map/reduce_scatter | solution.py:21
Sparse Core Ops, SparseCore 0:
  287.3 21.5 reduce-scatter.2
  311.7 75.4 reduce-scatter.4
